TPU v7x, 32 devices: a whole 2x2x4 slice. The times are simulated.
32 devices in a mesh: energy: 8 (over z, x), region: 4 (over y, core).
Axes of the slice: x: 2, y: 2, z: 4, core: 2. Of those that a mesh axis runs over, the one named last changes fastest.
Arguments:
- onsite: float32 [4, 2, 128, 128], P('region'), may hold values from -0.5 to 0.5
- coupling: float32 [4, 2, 128, 128], P('region'), may hold values from -0.044194174 to 1.5
- damping: float32 [4, 128], P('region'), may hold values from 0.1 to 0.25
- occupation: float32 [8, 4], P('energy', 'region'), may hold values from 0.05 to 0.95
- block_sizes: int32 [4], P('region'), may hold values from 64 to 128
- offsets: int32 [8], replicated, may hold values from -4 to 4
Outputs:
- pol: float32 [2, 8, 4, 96, 128], P(None, 'energy', 'region')
All inputs are finite; a program needn't handle non-finite values.
Results may differ from a plain program's by a relative error of at most 0.00085.
Values may be sent and summed in bfloat16 or wider, within the bound.
A program may use at most 64 MiB of HBM per device.

v0:
```python
import functools
import jax
import jax.numpy as jnp
from jax import lax
from jax.experimental import pallas as pl
from jax.experimental.pallas import tpu as pltpu
from jax.sharding import PartitionSpec as P

BAND = 96
PANEL = 8

energy_step = 0.1
left_lead = 0.5

VM = pl.BlockSpec(memory_space=pltpu.VMEM)
SM = pl.BlockSpec(memory_space=pltpu.SMEM)


def dot(x, y):
    return jnp.dot(x, y, precision=lax.Precision.HIGHEST, preferred_element_type=jnp.float32)


def halves(x):
    n = x.shape[-1] // 2
    return x[:, :n], x[:, n:]


def cat(re, im):
    return jnp.concatenate([re, im], axis=1)


def adjoint(x):
    re, im = halves(x)
    return cat(re.T, -im.T)


def cmul(x, y):
    re, im = halves(y)
    return dot(x, jnp.concatenate([y, cat(-im, re)], axis=0))


def lane_bcast(x, j):
    return jnp.broadcast_to(x[:, j : j + 1], x.shape)


def row_bcast(x, k):
    return jnp.broadcast_to(x[k : k + 1, :], x.shape)


def invert(a, rhs):
    n = a.shape[0]
    rhs[...] = jnp.zeros_like(rhs)
    lane = lax.broadcasted_iota(jnp.int32, (PANEL, n), 1)
    sub = lax.broadcasted_iota(jnp.int32, (PANEL, n), 0)
    wide = lax.broadcasted_iota(jnp.int32, (n, 2 * n), 1) % n

    def block(b, carry):
        start = pl.multiple_of(b * PANEL, PANEL)
        rows = pl.ds(start, PANEL)
        x = a[rows, :]
        xr, xi = halves(x)
        turn = (n - start) % n
        tr = pltpu.roll(xr, turn, 1)
        ti = pltpu.roll(xi, turn, 1)
        cols = [(lane_bcast(tr, j), lane_bcast(ti, j)) for j in range(PANEL)]
        inside = (lane >= start) & (lane < start + PANEL)
        cols.append(
            (
                jnp.where(inside, (lane - start == sub).astype(jnp.float32), xr),
                jnp.where(inside, 0.0, xi),
            )
        )
        for k in range(PANEL):
            br, bi = cols[k]
            pr, pi = row_bcast(br, k), row_bcast(bi, k)
            scale = 1.0 / (pr * pr + pi * pi)
            ir, ii = pr * scale, -pi * scale
            here = sub == k
            mr = jnp.where(here, -ir, br * ir - bi * ii)
            mi = jnp.where(here, -ii, br * ii + bi * ir)
            for j in range(k + 1, PANEL + 1):
                cr, ci = cols[j]
                rr, ri = row_bcast(cr, k), row_bcast(ci, k)
                cols[j] = (
                    jnp.where(here, 0.0, cr) - (mr * rr - mi * ri),
                    jnp.where(here, 0.0, ci) - (mr * ri + mi * rr),
                )
        zr, zi = cols[PANEL]
        low = pl.ds(pl.multiple_of(n + start, PANEL), PANEL)
        rhs[rows, :] = cat(zr, zi)
        rhs[low, :] = cat(-zi, zr)
        old = a[...]
        keep = (wide < start) | (wide >= start + PANEL)
        a[...] = jnp.where(keep, old, 0.0) - dot(old, rhs[...])
        a[rows, :] = cat(zr, zi)
        rhs[rows, :] = jnp.zeros((PANEL, 2 * n), jnp.float32)
        rhs[low, :] = jnp.zeros((PANEL, 2 * n), jnp.float32)
        return carry

    lax.fori_loop(0, n // PANEL, block, 0)


def build(regions, total, size, onsite, coupling, damping):
    n = onsite.shape[-1]
    row = lax.broadcasted_iota(jnp.int32, (n, n), 0)
    col = lax.broadcasted_iota(jnp.int32, (n, n), 1)
    mask = ((row < size) & (col < size)).astype(jnp.float32)
    eye = row == col
    region = lax.axis_index("region")
    energy = energy_step * (lax.axis_index("energy") - total // 2).astype(jnp.float32)
    o_re, o_im = onsite[0, 0], onsite[0, 1]
    h_re = 0.5 * (o_re + o_re.T) * mask
    h_im = 0.5 * (o_im - o_im.T) * mask
    u = cat(coupling[0, 0] * mask, coupling[0, 1] * mask)
    diag_im = jnp.broadcast_to(damping[...], (n, n)) + jnp.where(region == 0, left_lead, 0.0)
    a_re = jnp.where(eye, energy, 0.0) - h_re
    a_im = jnp.where(eye, diag_im, 0.0) - h_im
    return cat(a_re, a_im), u


def build_kernel(regions, total, sizes, onsite, coupling, damping, a_ref, u_ref):
    a, u = build(regions, total, sizes[0], onsite, coupling, damping)
    u_ref[...] = u
    a_ref[...] = a

    @pl.when(lax.axis_index("region") == regions - 1)
    def _():
        l_re, l_im = halves(cmul(u, adjoint(u)))
        a_ref[...] = a + cat(-l_im, l_re)


def step_kernel(a_ref, s_ref, w_ref, g_ref, out_ref, rhs):
    g_ref[...] = a_ref[...] - s_ref[...]
    invert(g_ref, rhs)
    w = w_ref[...]
    out_ref[...] = cmul(cmul(adjoint(w), g_ref[...]), w)


def back_kernel(g_ref, w_ref, after_ref, out_ref):
    g, w = g_ref[...], w_ref[...]
    out_ref[...] = g + cmul(cmul(cmul(g, w), after_ref[...]), cmul(adjoint(w), g))


def skew(t):
    n = t.shape[0]
    col = lax.broadcasted_iota(jnp.int32, (n, n), 1)
    bit = 1
    while bit < n:
        moved = jnp.concatenate([t[bit:], t[:bit]], axis=0)
        t = jnp.where((col // bit) % 2 == 1, moved, t)
        bit *= 2
    return t


def band_values(g, size, weight):
    re, im = halves(g)
    t_re = -(im + im.T)
    t_im = re.T - re
    n = re.shape[0]
    row = lax.broadcasted_iota(jnp.int32, (BAND, n), 0)
    col = lax.broadcasted_iota(jnp.int32, (BAND, n), 1)
    valid = (row + col < size).astype(jnp.float32)
    b_re = skew(t_re)[:BAND] * valid
    b_im = skew(t_im)[:BAND] * valid
    return [
        (weight * b_re),
        (weight * b_im),
        ((1.0 - weight) * b_re),
        ((1.0 - weight) * b_im),
    ]


def band_kernel(sizes, occ, g_ref, out_ref):
    count, rows = out_ref.shape[1], out_ref.shape[2]
    for c, v in enumerate(band_values(g_ref[...], sizes[0], occ[0, 0])):
        for e in range(count):
            out_ref[c, e] = v[e * rows : (e + 1) * rows].astype(jnp.bfloat16)


def pol_kernel(offsets, v_ref, out_ref):
    total = v_ref.shape[1]

    def one(k, carry):
        shape = v_ref.shape[2:]

        def term(e, acc):
            m = e - offsets[k]
            on = jnp.where((m >= 0) & (m < total), 1.0, 0.0)
            m = jnp.clip(m, 0, total - 1)
            lr = v_ref[0, e].astype(jnp.float32)
            li = v_ref[1, e].astype(jnp.float32)
            gr = v_ref[2, m].astype(jnp.float32) * on
            gi = v_ref[3, m].astype(jnp.float32) * on
            return (acc[0] + (lr * gr + li * gi), acc[1] + (li * gr - lr * gi))

        zero = jnp.zeros(shape, jnp.float32)
        re, im = lax.fori_loop(0, total, term, (zero, zero))
        out_ref[k, 0] = energy_step * re
        out_ref[k, 1] = energy_step * im
        return carry

    lax.fori_loop(0, out_ref.shape[0], one, 0)


def f32(*shape):
    return jax.ShapeDtypeStruct(shape, jnp.float32)


def local(onsite, coupling, damping, occupation, block_sizes, offsets):
    n = onsite.shape[-1]
    regions = lax.axis_size("region")
    total = lax.axis_size("energy")
    half = regions // 2
    pos = lax.axis_index("region")
    left = pos < half
    rows = BAND // total
    a, u = pl.pallas_call(
        functools.partial(build_kernel, regions, total),
        in_specs=[SM, VM, VM, VM],
        out_specs=[VM, VM],
        out_shape=[f32(n, 2 * n), f32(n, 2 * n)],
    )(block_sizes, onsite, coupling, damping)
    lower = lax.ppermute(u, "region", [(r, r + 1) for r in range(half - 1, regions - 1)])
    w = jnp.where(left, u, adjoint(lower))
    step = pl.pallas_call(
        step_kernel,
        in_specs=[VM, VM, VM],
        out_specs=[VM, VM],
        out_shape=[f32(n, 2 * n), f32(n, 2 * n)],
        scratch_shapes=[pltpu.VMEM((2 * n, 2 * n), jnp.float32)],
    )
    inward = [(r, r + 1) for r in range(half - 1)] + [(r, r - 1) for r in range(half + 1, regions)]
    sigma = jnp.zeros((n, 2 * n), jnp.float32)
    for s in range(half):
        g, out = step(a, sigma, w)
        if s < half - 1:
            sigma = lax.ppermute(out, "region", inward)
    middle = lax.ppermute(out, "region", [(half - 1, half), (half, half - 1)])
    full, _ = step(a, sigma + middle, w)
    outward = [(d, s) for s, d in inward]
    mid = (pos == half - 1) | (pos == half)
    back = pl.pallas_call(
        back_kernel, in_specs=[VM] * 3, out_specs=VM, out_shape=f32(n, 2 * n)
    )
    for s in range(half - 1):
        after = lax.ppermute(full, "region", outward)
        full = jnp.where(mid, full, back(g, w, after))
    packed = pl.pallas_call(
        band_kernel,
        in_specs=[SM, SM, VM],
        out_specs=VM,
        out_shape=jax.ShapeDtypeStruct((4, total, rows, n), jnp.bfloat16),
    )(block_sizes, occupation, full)
    moved = lax.all_to_all(packed, "energy", split_axis=1, concat_axis=1, tiled=True)
    freq = offsets.shape[0]
    res = pl.pallas_call(
        pol_kernel, in_specs=[SM, VM], out_specs=VM, out_shape=f32(freq, 2, rows, n)
    )(offsets, moved)
    res = lax.all_to_all(res, "energy", split_axis=0, concat_axis=0, tiled=True)
    res = res.reshape(total, freq // total, 2, rows, n)
    res = jnp.transpose(res, (2, 1, 0, 3, 4))
    return res.reshape(2, freq // total, 1, BAND, n)


def solution(mesh):
    placed = (
        P("region", None, None, None),
        P("region", None, None, None),
        P("region", None),
        P("energy", "region"),
        P("region"),
        P(),
    )
    return jax.shard_map(
        local,
        mesh=mesh,
        in_specs=placed,
        out_specs=P(None, "energy", "region", None, None),
        check_vma=False,
    )
```

profile of v0, /device:TPU:0, one launch (start us, length us, event | category | flops | bytes accessed | tf_op | source)
XLA Modules:
  0.0 96.8 jit_solution(16970237429901484200)
XLA Ops:
  0.7 1.8 %shard_map.64 = (f32[128,256]{1,0:T(8,128)}, f32[128,256]{1,0:T(8,128)}) custom-call(s32[1]{0:T(128)S(6)} %copy.17.sizes, f32[1,2,128,128]{3,2,1,0:T(8,128)} %onsite.1, f32[1,2,128,128]{3,2,1,0:T(8,128)} %coupling.1, f32[1,128]{1,0:T(1,128)} %damping.1), custom_call_target="tpu_custom_call" | custom-call | tf_op jit(solution)/shard_map/pallas_call | solution.py:217
  2.4 1.0 %copy.11 = f32[128,256]{0,1:T(8,128)S(1)} copy(f32[128,256]{1,0:T(8,128)} %get-tuple-element.12) | data formatting | bytes 262144 | tf_op jit(solution)/shard_map/pallas_call | solution.py:217
  3.4 0.7 collective-permute-start
  4.2 0.9 copy-done.1
  5.0 0.7 maximum_select_fusion.w_ref
  5.7 0.7 broadcast_in_dim.3.s_ref
  6.4 11.7 %shard_map.65 = (f32[128,256]{1,0:T(8,128)}, f32[128,256]{1,0:T(8,128)}) custom-call(f32[128,256]{1,0:T(8,128)} %get-tuple-element.11.a_ref, f32[128,256]{1,0:T(8,128)} %broadcast_in_dim.3.s_ref, f32[128,256]{1,0:T(8,128)} %maximum_select_fusion.w_ref), custom_call_target="tpu_custom_call" | custom-call | tf_op jit(solution)/shard_map/pallas_call | solution.py:235
  18.1 7.3 %collective-permute-start.1 = (f32[128,256]{1,0:T(8,128)}, f32[128,256]{1,0:T(8,128)S(1)}, u32[]{:S(2)}, u32[]{:S(2)}) collective-permute-start(f32[128,256]{1,0:T(8,128)} %get-tuple-element.13), channel_id=1, source_target_pairs={{0,1},{3,2},{4,5},{7,6},{8,9},{11,10},{12,13},{15,14},{16,17},{19,... | collective-permute-start | bytes 393224 | tf_op jit(solution)/shard_map/ppermute | solution.py:237
  25.4 1.2 %collective-permute-done.1.s_ref = f32[128,256]{1,0:T(8,128)S(1)} collective-permute-done((f32[128,256]{1,0:T(8,128)}, f32[128,256]{1,0:T(8,128)S(1)}, u32[]{:S(2)}, u32[]{:S(2)}) %collective-permute-start.1) | collective-permute-done | bytes 131104 | tf_op jit(solution)/shard_map/ppermute | solution.py:237
  27.2 11.7 %shard_map.66 = (f32[128,256]{1,0:T(8,128)}, f32[128,256]{1,0:T(8,128)}) custom-call(f32[128,256]{1,0:T(8,128)} %get-tuple-element.11.a_ref, f32[128,256]{1,0:T(8,128)} %copy-done, f32[128,256]{1,0:T(8,128)} %maximum_select_fusion.w_ref), custom_call_target="tpu_custom_call" | custom-call | tf_op jit(solution)/shard_map/pallas_call | solution.py:235
  38.9 0.7 collective-permute-start.2
  39.6 1.6 %add.3.s_ref = f32[128,256]{1,0:T(8,128)} add(f32[128,256]{1,0:T(8,128)} %copy-done, f32[128,256]{1,0:T(8,128)S(1)} %collective-permute-done.2) | non-fusion elementwise | flops 32768 | bytes 393216 | tf_op jit(solution)/shard_map/add | solution.py:239
  41.2 11.7 %shard_map.67 = (f32[128,256]{1,0:T(8,128)}, f32[128,256]{1,0:T(8,128)}) custom-call(f32[128,256]{1,0:T(8,128)} %get-tuple-element.11.a_ref, f32[128,256]{1,0:T(8,128)} %add.3.s_ref, f32[128,256]{1,0:T(8,128)} %maximum_select_fusion.w_ref), custom_call_target="tpu_custom_call" | custom-call | tf_op jit(solution)/shard_map/pallas_call | solution.py:239
  52.9 1.3 %collective-permute-start.3 = (f32[128,256]{1,0:T(8,128)}, f32[128,256]{1,0:T(8,128)S(1)}, u32[]{:S(2)}, u32[]{:S(2)}) collective-permute-start(f32[128,256]{1,0:T(8,128)} %get-tuple-element.15), channel_id=1, source_target_pairs={{1,0},{2,3},{5,4},{6,7},{9,8},{10,11},{13,12},{14,15},{17,16},{18,... | collective-permute-start | bytes 393224 | tf_op jit(solution)/shard_map/ppermute | solution.py:246
  54.8 7.3 %collective-permute-done.3.after_ref = f32[128,256]{1,0:T(8,128)S(1)} collective-permute-done((f32[128,256]{1,0:T(8,128)}, f32[128,256]{1,0:T(8,128)S(1)}, u32[]{:S(2)}, u32[]{:S(2)}) %collective-permute-start.3) | collective-permute-done | bytes 131104 | tf_op jit(solution)/shard_map/ppermute | solution.py:246
  62.7 2.7 %shard_map.68 = f32[128,256]{1,0:T(8,128)} custom-call(f32[128,256]{1,0:T(8,128)} %get-tuple-element.16.g_ref, f32[128,256]{1,0:T(8,128)} %maximum_select_fusion.w_ref, f32[128,256]{1,0:T(8,128)} %copy-done.3), custom_call_target="tpu_custom_call" | custom-call | tf_op jit(solution)/shard_map/pallas_call | solution.py:247
  65.4 1.6 %broadcast_select_fusion.g_ref = f32[128,256]{1,0:T(8,128)} fusion(f32[128,256]{1,0:T(8,128)S(1)} %copy-done.2, f32[128,256]{1,0:T(8,128)} %shard_map.68, pred[]{:T(512)S(6)} %or.3), kind=kLoop, calls=%fused_computation.4 | loop fusion | flops 32768 | bytes 393217 | tf_op jit(solution)/shard_map/jit(_where)/select_n | solution.py:247
  67.0 1.7 %shard_map.69 = bf16[4,8,12,128]{3,2,1,0:T(8,128)(2,1)} custom-call(s32[1]{0:T(128)S(6)} %copy.17.sizes, f32[1,1]{1,0:T(1,128)S(6)} %copy.16.occ, f32[128,256]{1,0:T(8,128)} %broadcast_select_fusion.g_ref), custom_call_target="tpu_custom_call" | custom-call | tf_op jit(solution)/shard_map/pallas_call | solution.py:248
  68.7 1.0 %copy.12 = bf16[4,8,12,128]{3,0,2,1:T(4,128)(2,1)S(1)} copy(bf16[4,8,12,128]{3,2,1,0:T(8,128)(2,1)} %shard_map.69) | data formatting | bytes 196608 | tf_op jit(solution)/shard_map/pallas_call | solution.py:248
  69.7 12.7 %all_to_all.10 = bf16[4,8,12,128]{3,0,2,1:T(4,128)(2,1)S(1)} all-to-all(bf16[4,8,12,128]{3,0,2,1:T(4,128)(2,1)S(1)} %copy.12), channel_id=1, replica_groups=mesh['energy'=8,'region'=4] {'energy'}, dimensions={1} | all-to-all | bytes 196608 | tf_op jit(solution)/shard_map/all_to_all | solution.py:254
  82.4 0.7 copy.13.v_ref
  83.1 2.6 %shard_map.70 = f32[8,2,12,128]{3,2,1,0:T(8,128)} custom-call(s32[8]{0:T(128)} %offsets.1, bf16[4,8,12,128]{3,2,1,0:T(8,128)(2,1)} %copy.13.v_ref), custom_call_target="tpu_custom_call" | custom-call | tf_op jit(solution)/shard_map/pallas_call | solution.py:256
  85.6 1.0 copy.14
  86.6 9.5 %all_to_all.11 = f32[8,2,12,128]{3,1,2,0:T(2,128)S(1)} all-to-all(f32[8,2,12,128]{3,1,2,0:T(2,128)S(1)} %copy.14), channel_id=1, replica_groups=mesh['energy'=8,'region'=4] {'energy'}, dimensions={0} | all-to-all | bytes 196608 | tf_op jit(solution)/shard_map/all_to_all | solution.py:259
  (11 shorter events, 2.0 us)
Async XLA Ops:
  3.4 0.7 collective-permute-start
  4.1 0.9 copy-start.1
  18.1 8.5 %collective-permute-start.1 = (f32[128,256]{1,0:T(8,128)}, f32[128,256]{1,0:T(8,128)S(1)}, u32[]{:S(2)}, u32[]{:S(2)}) collective-permute-start(f32[128,256]{1,0:T(8,128)} %get-tuple-element.13), channel_id=1, source_target_pairs={{0,1},{3,2},{4,5},{7,6},{8,9},{11,10},{12,13},{15,14},{16,17},{19,... | collective-permute-start | bytes 393224 | tf_op jit(solution)/shard_map/ppermute | solution.py:237
  26.6 0.6 copy-start
  38.9 0.7 collective-permute-start.2
  52.9 9.2 %collective-permute-start.3 = (f32[128,256]{1,0:T(8,128)}, f32[128,256]{1,0:T(8,128)S(1)}, u32[]{:S(2)}, u32[]{:S(2)}) collective-permute-start(f32[128,256]{1,0:T(8,128)} %get-tuple-element.15), channel_id=1, source_target_pairs={{1,0},{2,3},{5,4},{6,7},{9,8},{10,11},{13,12},{14,15},{17,16},{18,... | collective-permute-start | bytes 393224 | tf_op jit(solution)/shard_map/ppermute | solution.py:246
  62.1 0.7 copy-start.3
  62.7 2.7 %copy-start.2 = (f32[128,256]{1,0:T(8,128)S(1)}, f32[128,256]{1,0:T(8,128)}, u32[]{:S(2)}) copy-start(f32[128,256]{1,0:T(8,128)} %get-tuple-element.15) | copy-start | bytes 393220
where the time goes:
time: 97.3 us; the launch traced here: 96.8 us
  Pallas kernels  43.9 us (45%)
  blocking collectives  22.2 us (23%)
  starting transfers between devices  9.89 us (10%)
  waiting for transfers between devices  8.43 us (9%)
  local copies, waits for them, and re-layouts  7.09 us (7%)
  other arithmetic  3.82 us (4%)
  between operations  1.4 us (1%)
    pallas_call x2, Pallas kernels, local(): g, out = step(a, sigma, w)  23.4 us
    all_to_all x1, blocking collectives, local(): lax.all_to_all(packed, 'energy', split_axis=1, concat_axis=1, tiled=True)  12.7 us
    pallas_call x1, Pallas kernels, local(): full, _ = step(a, sigma + middle, w)  11.7 us
    all_to_all x1, blocking collectives, local(): res = lax.all_to_all(res, 'energy', split_axis=0, concat_axis=0, tiled=True)  9.51 us
    ppermute x1, starting transfers between devices, local(): sigma = lax.ppermute(out, 'region', inward)  7.29 us
    ppermute x1, waiting for transfers between devices, local(): after = lax.ppermute(full, 'region', outward)  7.25 us
    pallas_call x1, Pallas kernels, local(): full = jnp.where(mid, full, back(g, w, after))  2.65 us
    pallas_call x1, Pallas kernels, local(): pl.pallas_call(pol_kernel, in_specs=[SM, VM], out_specs=VM, out_shape=f32...  2.57 us
  transfers between devices with their start and end apart: 4, of which 2 were waited for; matrix products, arithmetic and copies ran while one was open for 0% of the time, Pallas kernels for 0%

commit v1 on v0

--- a/solution.py
+++ b/solution.py
@@ -118,29 +118,6 @@
     return cat(a_re, a_im), u
 
 
-def build_kernel(regions, total, sizes, onsite, coupling, damping, a_ref, u_ref):
-    a, u = build(regions, total, sizes[0], onsite, coupling, damping)
-    u_ref[...] = u
-    a_ref[...] = a
-
-    @pl.when(lax.axis_index("region") == regions - 1)
-    def _():
-        l_re, l_im = halves(cmul(u, adjoint(u)))
-        a_ref[...] = a + cat(-l_im, l_re)
-
-
-def step_kernel(a_ref, s_ref, w_ref, g_ref, out_ref, rhs):
-    g_ref[...] = a_ref[...] - s_ref[...]
-    invert(g_ref, rhs)
-    w = w_ref[...]
-    out_ref[...] = cmul(cmul(adjoint(w), g_ref[...]), w)
-
-
-def back_kernel(g_ref, w_ref, after_ref, out_ref):
-    g, w = g_ref[...], w_ref[...]
-    out_ref[...] = g + cmul(cmul(cmul(g, w), after_ref[...]), cmul(adjoint(w), g))
-
-
 def skew(t):
     n = t.shape[0]
     col = lax.broadcasted_iota(jnp.int32, (n, n), 1)
@@ -170,96 +147,229 @@
     ]
 
 
-def band_kernel(sizes, occ, g_ref, out_ref):
-    count, rows = out_ref.shape[1], out_ref.shape[2]
-    for c, v in enumerate(band_values(g_ref[...], sizes[0], occ[0, 0])):
-        for e in range(count):
-            out_ref[c, e] = v[e * rows : (e + 1) * rows].astype(jnp.bfloat16)
-
-
-def pol_kernel(offsets, v_ref, out_ref):
-    total = v_ref.shape[1]
-
-    def one(k, carry):
-        shape = v_ref.shape[2:]
+def send(src, dst, sems, axis, index):
+    return pltpu.make_async_remote_copy(
+        src_ref=src,
+        dst_ref=dst,
+        send_sem=sems[0],
+        recv_sem=sems[1],
+        device_id={axis: index},
+        device_id_type=pl.DeviceIdType.MESH,
+    )
+
+
+def kernel(
+    regions, peers, sizes, occ, offsets, onsite, coupling, damping, out_ref,
+    a, g, w, u, u_in, s_out, s_in, m_out, m_in, g_in, full, rhs,
+    band_out, band_in, pol_out, pol_in,
+    link_send, link_recv, band_send, band_recv, pol_send, pol_recv,
+):
+    half = regions // 2
+    pos = lax.axis_index("region")
+    me = lax.axis_index("energy")
+    left = pos < half
+    inner = jnp.where(left, pos + 1, pos - 1)
+    outer = jnp.where(left, pos - 1, pos + 1)
+    is_mid = (pos == half - 1) | (pos == half)
+    is_end = (pos == 0) | (pos == regions - 1)
+
+    barrier = pltpu.get_barrier_semaphore()
+
+    def greet(axis, index):
+        pl.semaphore_signal(
+            barrier, inc=1, device_id={axis: index}, device_id_type=pl.DeviceIdType.MESH
+        )
+
+    greet("region", inner)
+
+    @pl.when(jnp.logical_not(is_end))
+    def _():
+        greet("region", outer)
+
+    def greet_peer(j, carry):
+        greet("energy", lax.rem(me + j, peers))
+        return carry
+
+    lax.fori_loop(1, peers, greet_peer, 0)
+
+    a0, u0 = build(regions, peers, sizes[0], onsite, coupling, damping)
+    u[...] = u0
+    w[...] = u0
+    a[...] = a0
+
+    @pl.when(is_end)
+    def _():
+        pl.semaphore_wait(barrier, peers)
+
+    @pl.when(jnp.logical_not(is_end))
+    def _():
+        pl.semaphore_wait(barrier, peers + 1)
+
+    def link(i, src, dst, index):
+        return send(src, dst, (link_send.at[i], link_recv.at[i]), "region", index)
+
+    gives = (pos >= half - 1) & (pos < regions - 1)
+
+    @pl.when(gives)
+    def _():
+        link(0, u, u_in, pos + 1).start()
+
+    @pl.when(pos == regions - 1)
+    def _():
+        l_re, l_im = halves(cmul(u0, adjoint(u0)))
+        a[...] = a0 + cat(-l_im, l_re)
+
+    @pl.when(jnp.logical_not(is_end))
+    def _():
+        link(1, s_out, s_in, outer).wait_recv()
+        a[...] = a[...] - s_in[...]
+
+    g[...] = a[...]
+    invert(g, rhs)
+
+    @pl.when(jnp.logical_not(left))
+    def _():
+        link(0, u, u_in, pos - 1).wait_recv()
+        w[...] = adjoint(u_in[...])
+
+    @pl.when(is_mid)
+    def _():
+        wv = w[...]
+        m_out[...] = cmul(cmul(adjoint(wv), g[...]), wv)
+        copy = link(2, m_out, m_in, inner)
+        copy.start()
+        copy.wait_recv()
+        full[...] = a[...] - m_in[...]
+        invert(full, rhs)
+        copy.wait_send()
+
+    @pl.when(jnp.logical_not(is_mid))
+    def _():
+        wv = w[...]
+        wg = cmul(adjoint(wv), g[...])
+        s_out[...] = cmul(wg, wv)
+        copy = link(1, s_out, s_in, inner)
+        copy.start()
+        gw = cmul(g[...], wv)
+        link(3, full, g_in, inner).wait_recv()
+        full[...] = g[...] + cmul(cmul(gw, g_in[...]), wg)
+        copy.wait_send()
+
+    @pl.when(jnp.logical_not(is_end))
+    def _():
+        link(3, full, g_in, outer).start()
+
+    rows = BAND // peers
+    n = onsite.shape[-1]
+    for c, v in enumerate(band_values(full[...], sizes[0], occ[0, 0])):
+        v = v.astype(jnp.bfloat16)
+        for e in range(peers):
+            band_out[e, c] = v[e * rows : (e + 1) * rows]
+
+    def band_copy(j):
+        peer = lax.rem(me + j, peers)
+        return send(
+            band_out.at[peer], band_in.at[me], (band_send.at[j], band_recv.at[j]), "energy", peer
+        )
+
+    def each(make, act):
+        def one(j, carry):
+            act(make(j))
+            return carry
+
+        lax.fori_loop(1, peers, one, 0)
+
+    each(band_copy, lambda c: c.start())
+    band_in[me] = band_out[me]
+    each(band_copy, lambda c: c.wait_recv())
+
+    kept = offsets.shape[0] // peers
+
+    def pol_copy(j):
+        peer = lax.rem(me + j, peers)
+        return send(
+            pol_out.at[peer], pol_in.at[me], (pol_send.at[j], pol_recv.at[j]), "energy", peer
+        )
+
+    def frequency(owner, i):
+        offset = offsets[owner * kept + i]
 
         def term(e, acc):
-            m = e - offsets[k]
-            on = jnp.where((m >= 0) & (m < total), 1.0, 0.0)
-            m = jnp.clip(m, 0, total - 1)
-            lr = v_ref[0, e].astype(jnp.float32)
-            li = v_ref[1, e].astype(jnp.float32)
-            gr = v_ref[2, m].astype(jnp.float32) * on
-            gi = v_ref[3, m].astype(jnp.float32) * on
+            m = e - offset
+            on = jnp.where((m >= 0) & (m < peers), 1.0, 0.0)
+            m = jnp.clip(m, 0, peers - 1)
+            lr = band_in[e, 0].astype(jnp.float32)
+            li = band_in[e, 1].astype(jnp.float32)
+            gr = band_in[m, 2].astype(jnp.float32) * on
+            gi = band_in[m, 3].astype(jnp.float32) * on
             return (acc[0] + (lr * gr + li * gi), acc[1] + (li * gr - lr * gi))
 
-        zero = jnp.zeros(shape, jnp.float32)
-        re, im = lax.fori_loop(0, total, term, (zero, zero))
-        out_ref[k, 0] = energy_step * re
-        out_ref[k, 1] = energy_step * im
+        acc = (jnp.zeros((rows, n), jnp.float32), jnp.zeros((rows, n), jnp.float32))
+        if peers <= 16:
+            for e in range(peers):
+                acc = term(e, acc)
+        else:
+            acc = lax.fori_loop(0, peers, term, acc)
+        return energy_step * acc[0], energy_step * acc[1]
+
+    def owned(j, carry):
+        owner = lax.rem(me + j, peers)
+        for i in range(kept):
+            re, im = frequency(owner, i)
+            pol_out[owner, i, 0] = re
+            pol_out[owner, i, 1] = im
+
+        pol_copy(j).start()
         return carry
 
-    lax.fori_loop(0, out_ref.shape[0], one, 0)
-
-
-def f32(*shape):
-    return jax.ShapeDtypeStruct(shape, jnp.float32)
+    lax.fori_loop(1, peers, owned, 0)
+    for i in range(kept):
+        re, im = frequency(me, i)
+        pol_in[me, i, 0] = re
+        pol_in[me, i, 1] = im
+    each(pol_copy, lambda c: c.wait_recv())
+    for e in range(peers):
+        for i in range(kept):
+            for c in range(2):
+                out_ref[c, i, 0, e * rows : (e + 1) * rows, :] = pol_in[e, i, c]
+
+    each(band_copy, lambda c: c.wait_send())
+    each(pol_copy, lambda c: c.wait_send())
+
+    @pl.when(gives)
+    def _():
+        link(0, u, u_in, pos + 1).wait_send()
+
+    @pl.when(jnp.logical_not(is_end))
+    def _():
+        link(3, full, g_in, outer).wait_send()
 
 
 def local(onsite, coupling, damping, occupation, block_sizes, offsets):
     n = onsite.shape[-1]
     regions = lax.axis_size("region")
-    total = lax.axis_size("energy")
-    half = regions // 2
-    pos = lax.axis_index("region")
-    left = pos < half
-    rows = BAND // total
-    a, u = pl.pallas_call(
-        functools.partial(build_kernel, regions, total),
-        in_specs=[SM, VM, VM, VM],
-        out_specs=[VM, VM],
-        out_shape=[f32(n, 2 * n), f32(n, 2 * n)],
-    )(block_sizes, onsite, coupling, damping)
-    lower = lax.ppermute(u, "region", [(r, r + 1) for r in range(half - 1, regions - 1)])
-    w = jnp.where(left, u, adjoint(lower))
-    step = pl.pallas_call(
-        step_kernel,
-        in_specs=[VM, VM, VM],
-        out_specs=[VM, VM],
-        out_shape=[f32(n, 2 * n), f32(n, 2 * n)],
-        scratch_shapes=[pltpu.VMEM((2 * n, 2 * n), jnp.float32)],
-    )
-    inward = [(r, r + 1) for r in range(half - 1)] + [(r, r - 1) for r in range(half + 1, regions)]
-    sigma = jnp.zeros((n, 2 * n), jnp.float32)
-    for s in range(half):
-        g, out = step(a, sigma, w)
-        if s < half - 1:
-            sigma = lax.ppermute(out, "region", inward)
-    middle = lax.ppermute(out, "region", [(half - 1, half), (half, half - 1)])
-    full, _ = step(a, sigma + middle, w)
-    outward = [(d, s) for s, d in inward]
-    mid = (pos == half - 1) | (pos == half)
-    back = pl.pallas_call(
-        back_kernel, in_specs=[VM] * 3, out_specs=VM, out_shape=f32(n, 2 * n)
-    )
-    for s in range(half - 1):
-        after = lax.ppermute(full, "region", outward)
-        full = jnp.where(mid, full, back(g, w, after))
-    packed = pl.pallas_call(
-        band_kernel,
-        in_specs=[SM, SM, VM],
+    peers = lax.axis_size("energy")
+    rows = BAND // peers
+    kept = offsets.shape[0] // peers
+    block = pltpu.VMEM((n, 2 * n), jnp.float32)
+    return pl.pallas_call(
+        functools.partial(kernel, regions, peers),
+        in_specs=[SM, SM, SM, VM, VM, VM],
         out_specs=VM,
-        out_shape=jax.ShapeDtypeStruct((4, total, rows, n), jnp.bfloat16),
-    )(block_sizes, occupation, full)
-    moved = lax.all_to_all(packed, "energy", split_axis=1, concat_axis=1, tiled=True)
-    freq = offsets.shape[0]
-    res = pl.pallas_call(
-        pol_kernel, in_specs=[SM, VM], out_specs=VM, out_shape=f32(freq, 2, rows, n)
-    )(offsets, moved)
-    res = lax.all_to_all(res, "energy", split_axis=0, concat_axis=0, tiled=True)
-    res = res.reshape(total, freq // total, 2, rows, n)
-    res = jnp.transpose(res, (2, 1, 0, 3, 4))
-    return res.reshape(2, freq // total, 1, BAND, n)
+        out_shape=jax.ShapeDtypeStruct((2, kept, 1, BAND, n), jnp.float32),
+        scratch_shapes=[block] * 11
+        + [
+            pltpu.VMEM((2 * n, 2 * n), jnp.float32),
+            pltpu.VMEM((peers, 4, rows, n), jnp.bfloat16),
+            pltpu.VMEM((peers, 4, rows, n), jnp.bfloat16),
+            pltpu.VMEM((peers, kept, 2, rows, n), jnp.float32),
+            pltpu.VMEM((peers, kept, 2, rows, n), jnp.float32),
+            pltpu.SemaphoreType.DMA((4,)),
+            pltpu.SemaphoreType.DMA((4,)),
+        ]
+        + [pltpu.SemaphoreType.DMA((peers,))] * 4,
+        compiler_params=pltpu.CompilerParams(collective_id=0, has_side_effects=True),
+    )(block_sizes, occupation, offsets, onsite, coupling, damping)
 
 
 def solution(mesh):

time: 97.3 us -> 57.4 us (0.59)
  blocking collectives: 22.2 us -> 0 us
  Pallas kernels: 43.9 us -> 54.3 us
  starting transfers between devices: 9.89 us -> 0 us
  waiting for transfers between devices: 8.43 us -> 0 us
  local copies, waits for them, and re-layouts: 7.09 us -> 1.54 us
  other arithmetic: 3.82 us -> 0 us
    all_to_all x2 -> x0, blocking collectives: 22.2 us -> none  [the longest x1 12.7 us: local(): lax.all_to_all(packed, 'energy', split_axis=1, concat_axis=1, tiled=True)]
    pallas_call x7 -> x1, Pallas kernels: 43.9 us -> 54.3 us  [local(): pl.pallas_call(functools.partial(kernel, regions, peers), in_specs=[SM, S...]
    ppermute x4 -> x0, starting transfers between devices: 9.89 us -> none  [the longest x1 7.29 us: local(): sigma = lax.ppermute(out, 'region', inward)]
    ppermute x4 -> x0, waiting for transfers between devices: 8.43 us -> none  [the longest x1 7.25 us: local(): after = lax.ppermute(full, 'region', outward)]
    pallas_call x3 -> x0, local copies, waits for them, and re-layouts: 2.93 us -> none  [the longest x1 0.99 us: local(): pl.pallas_call(functools.partial(build_kernel, regions, total), in_specs=...]
    select_n x2 -> x0, other arithmetic: 2.23 us -> none  [the longest x1 1.57 us: local(): full = jnp.where(mid, full, back(g, w, after))]
    add x1 -> x0, other arithmetic: 1.58 us -> none  [local(): full, _ = step(a, sigma + middle, w)]
    unnamed x8 -> x1, local copies, waits for them, and re-layouts: 2.17 us -> 1.54 us
  transfers between devices with their start and end apart: 4 -> 0, of which waited for: 2 -> 0; matrix products, arithmetic and copies ran while one was open for 0% -> 0% of each run, Pallas kernels for 0% -> 0%
where the time goes in v1:
time: 57.4 us; the launch traced here: 57.2 us
  Pallas kernels  54.3 us (95%)
  local copies, waits for them, and re-layouts  1.54 us (3%)
  between operations  1.3 us (2%)
    pallas_call x1, Pallas kernels, local(): pl.pallas_call(functools.partial(kernel, regions, peers), in_specs=[SM, S...  54.3 us
    unnamed x1, local copies, waits for them, and re-layouts  1.54 us

profile of v1, /device:TPU:0, one launch (start us, length us, event | category | flops | bytes accessed | tf_op | source)
XLA Modules:
  0.0 57.2 jit_solution(4698905433768192072)
XLA Ops:
  1.3 54.3 %shard_map.64 = f32[2,1,1,96,128]{4,3,2,1,0:T(8,128)} custom-call(s32[1]{0:T(128)S(6)} %copy.9.sizes, f32[1,1]{1,0:T(1,128)S(6)} %copy.8.occ, s32[8]{0:T(128)} %offsets.1, f32[1,2,128,128]{3,2,1,0:T(8,128)} %onsite.1, f32[1,2,128,128]{3,2,1,0:T(8,128)} %coupling.1, f32[1,128]{1,0:T(1,128)} %damping.1), custom_call_target="tpu_custom_call" | custom-call | tf_op jit(solution)/shard_map/pallas_call | solution.py:355
  55.6 1.5 %copy.10 = f32[2,1,1,96,128]{4,3,2,1,0:T(8,128)} copy(f32[2,1,1,96,128]{4,3,2,1,0:T(8,128)} %shard_map.64) | data formatting | bytes 196608

commit v2 on v1

--- a/solution.py
+++ b/solution.py
@@ -47,57 +47,92 @@
     return jnp.broadcast_to(x[k : k + 1, :], x.shape)
 
 
+def factor(x, start):
+    xr, xi = x
+    n = xr.shape[1]
+    lane = lax.broadcasted_iota(jnp.int32, (PANEL, n), 1) - start
+    sub = lax.broadcasted_iota(jnp.int32, (PANEL, n), 0)
+    turn = (n - start) % n
+    tr = pltpu.roll(xr, turn, 1)
+    ti = pltpu.roll(xi, turn, 1)
+    cols = [(lane_bcast(tr, j), lane_bcast(ti, j)) for j in range(PANEL)]
+    inside = (lane >= 0) & (lane < PANEL)
+    cols.append((jnp.where(inside, (lane == sub).astype(jnp.float32), xr), jnp.where(inside, 0.0, xi)))
+    for k in range(PANEL):
+        br, bi = cols[k]
+        pr, pi = row_bcast(br, k), row_bcast(bi, k)
+        scale = 1.0 / (pr * pr + pi * pi)
+        here = sub == k
+        qr = jnp.where(here, -pr, br * pr + bi * pi)
+        qi = jnp.where(here, pi, bi * pr - br * pi)
+        mr, mi = qr * scale, qi * scale
+        for j in range(k + 1, PANEL + 1):
+            cr, ci = cols[j]
+            rr, ri = row_bcast(cr, k), row_bcast(ci, k)
+            cols[j] = (
+                jnp.where(here, 0.0, cr) - (mr * rr - mi * ri),
+                jnp.where(here, 0.0, ci) - (mr * ri + mi * rr),
+            )
+    return cols[PANEL]
+
 def invert(a, rhs):
     n = a.shape[0]
     rhs[...] = jnp.zeros_like(rhs)
     lane = lax.broadcasted_iota(jnp.int32, (PANEL, n), 1)
-    sub = lax.broadcasted_iota(jnp.int32, (PANEL, n), 0)
     wide = lax.broadcasted_iota(jnp.int32, (n, 2 * n), 1) % n
-
-    def block(b, carry):
+    zero = jnp.zeros((PANEL, 2 * n), jnp.float32)
+
+    def places(start):
+        return pl.ds(start, PANEL), pl.ds(pl.multiple_of(n + start, PANEL), PANEL)
+
+    def put(start, z):
+        rows, low = places(start)
+        rhs[rows, :] = cat(z[0], z[1])
+        rhs[low, :] = cat(-z[1], z[0])
+
+    def updated(start):
+        old = a[...]
+        keep = (wide < start) | (wide >= start + PANEL)
+        return jnp.where(keep, old, 0.0) - dot(old, rhs[...])
+
+    def clear(start):
+        rows, low = places(start)
+        rhs[rows, :] = zero
+        rhs[low, :] = zero
+
+    first = factor(halves(a[:PANEL, :]), 0)
+    put(0, first)
+
+    def block(b, z):
+        last = pl.multiple_of((b - 1) * PANEL, PANEL)
         start = pl.multiple_of(b * PANEL, PANEL)
-        rows = pl.ds(start, PANEL)
-        x = a[rows, :]
-        xr, xi = halves(x)
-        turn = (n - start) % n
+        new = updated(last)
+        xr, xi = halves(a[pl.ds(start, PANEL), :])
+        turn = (n - last) % n
         tr = pltpu.roll(xr, turn, 1)
         ti = pltpu.roll(xi, turn, 1)
-        cols = [(lane_bcast(tr, j), lane_bcast(ti, j)) for j in range(PANEL)]
-        inside = (lane >= start) & (lane < start + PANEL)
-        cols.append(
-            (
-                jnp.where(inside, (lane - start == sub).astype(jnp.float32), xr),
-                jnp.where(inside, 0.0, xi),
-            )
-        )
-        for k in range(PANEL):
-            br, bi = cols[k]
-            pr, pi = row_bcast(br, k), row_bcast(bi, k)
-            scale = 1.0 / (pr * pr + pi * pi)
-            ir, ii = pr * scale, -pi * scale
-            here = sub == k
-            mr = jnp.where(here, -ir, br * ir - bi * ii)
-            mi = jnp.where(here, -ii, br * ii + bi * ir)
-            for j in range(k + 1, PANEL + 1):
-                cr, ci = cols[j]
-                rr, ri = row_bcast(cr, k), row_bcast(ci, k)
-                cols[j] = (
-                    jnp.where(here, 0.0, cr) - (mr * rr - mi * ri),
-                    jnp.where(here, 0.0, ci) - (mr * ri + mi * rr),
-                )
-        zr, zi = cols[PANEL]
-        low = pl.ds(pl.multiple_of(n + start, PANEL), PANEL)
-        rhs[rows, :] = cat(zr, zi)
-        rhs[low, :] = cat(-zi, zr)
-        old = a[...]
-        keep = (wide < start) | (wide >= start + PANEL)
-        a[...] = jnp.where(keep, old, 0.0) - dot(old, rhs[...])
-        a[rows, :] = cat(zr, zi)
-        rhs[rows, :] = jnp.zeros((PANEL, 2 * n), jnp.float32)
-        rhs[low, :] = jnp.zeros((PANEL, 2 * n), jnp.float32)
-        return carry
-
-    lax.fori_loop(0, n // PANEL, block, 0)
+        inside = (lane >= last) & (lane < last + PANEL)
+        xr = jnp.where(inside, 0.0, xr)
+        xi = jnp.where(inside, 0.0, xi)
+        accs=[]
+        for j in range(PANEL):
+            cr, ci = lane_bcast(tr, j), lane_bcast(ti, j)
+            rr, ri = row_bcast(z[0], j), row_bcast(z[1], j)
+            accs.append((cr * rr - ci * ri, cr * ri + ci * rr))
+        while len(accs)>1:
+            accs=[(p[0]+q[0],p[1]+q[1]) for p,q in zip(accs[::2],accs[1::2])]
+        xr, xi = xr-accs[0][0], xi-accs[0][1]
+        fresh = factor((xr, xi), start)
+        a[...] = new
+        a[pl.ds(last, PANEL), :] = cat(z[0], z[1])
+        clear(last)
+        put(start, fresh)
+        return fresh
+
+    z = lax.fori_loop(1, n // PANEL, block, first)
+    last = n - PANEL
+    a[...] = updated(last)
+    a[pl.ds(last, PANEL), :] = cat(z[0], z[1])
 
 
 def build(regions, total, size, onsite, coupling, damping):
@@ -197,19 +232,17 @@
     w[...] = u0
     a[...] = a0
 
-    @pl.when(is_end)
-    def _():
-        pl.semaphore_wait(barrier, peers)
-
-    @pl.when(jnp.logical_not(is_end))
-    def _():
-        pl.semaphore_wait(barrier, peers + 1)
+    gives = (pos >= half - 1) & (pos < regions - 1)
+    early = jnp.logical_not(is_end) | gives
+
+    def enter():
+        pl.semaphore_wait(barrier, jnp.where(is_end, peers, peers + 1))
+
+    pl.when(early)(enter)
 
     def link(i, src, dst, index):
         return send(src, dst, (link_send.at[i], link_recv.at[i]), "region", index)
 
-    gives = (pos >= half - 1) & (pos < regions - 1)
-
     @pl.when(gives)
     def _():
         link(0, u, u_in, pos + 1).start()
@@ -222,13 +255,29 @@
     @pl.when(jnp.logical_not(is_end))
     def _():
         link(1, s_out, s_in, outer).wait_recv()
-        a[...] = a[...] - s_in[...]
+
+        @pl.when(left)
+        def _():
+            a[...] = a[...] - s_in[...]
+
+        @pl.when(jnp.logical_not(left))
+        def _():
+            uv = u[...]
+            a[...] = a[...] - cmul(cmul(uv, s_in[...]), adjoint(uv))
 
     g[...] = a[...]
     invert(g, rhs)
+    pl.when(jnp.logical_not(early))(enter)
+
+    own = link(1, s_out, s_in, inner)
 
     @pl.when(jnp.logical_not(left))
     def _():
+        @pl.when(jnp.logical_not(is_mid))
+        def _():
+            s_out[...] = g[...]
+            own.start()
+
         link(0, u, u_in, pos - 1).wait_recv()
         w[...] = adjoint(u_in[...])
 
@@ -247,13 +296,16 @@
     def _():
         wv = w[...]
         wg = cmul(adjoint(wv), g[...])
-        s_out[...] = cmul(wg, wv)
-        copy = link(1, s_out, s_in, inner)
-        copy.start()
+
+        @pl.when(left)
+        def _():
+            s_out[...] = cmul(wg, wv)
+            own.start()
+
         gw = cmul(g[...], wv)
         link(3, full, g_in, inner).wait_recv()
         full[...] = g[...] + cmul(cmul(gw, g_in[...]), wg)
-        copy.wait_send()
+        own.wait_send()
 
     @pl.when(jnp.logical_not(is_end))
     def _():

time: 57.4 us -> 47.5 us (0.83)
  Pallas kernels: 54.3 us -> 44.4 us
    pallas_call x1, Pallas kernels: 54.3 us -> 44.4 us  [local(): pl.pallas_call(functools.partial(kernel, regions, peers), in_specs=[SM, S...]
where the time goes in v2:
time: 47.5 us; the launch traced here: 47.3 us
  Pallas kernels  44.4 us (93%)
  local copies, waits for them, and re-layouts  1.54 us (3%)
  between operations  1.3 us (3%)
    pallas_call x1, Pallas kernels, local(): pl.pallas_call(functools.partial(kernel, regions, peers), in_specs=[SM, S...  44.4 us
    unnamed x1, local copies, waits for them, and re-layouts  1.54 us

profile of v2, /device:TPU:0, one launch (start us, length us, event | category | flops | bytes accessed | tf_op | source)
XLA Modules:
  0.0 47.3 jit_solution(11181794106065843417)
XLA Ops:
  1.3 44.4 %shard_map.64 = f32[2,1,1,96,128]{4,3,2,1,0:T(8,128)} custom-call(s32[1]{0:T(128)S(6)} %copy.9.sizes, f32[1,1]{1,0:T(1,128)S(6)} %copy.8.occ, s32[8]{0:T(128)} %offsets.1, f32[1,2,128,128]{3,2,1,0:T(8,128)} %onsite.1, f32[1,2,128,128]{3,2,1,0:T(8,128)} %coupling.1, f32[1,128]{1,0:T(1,128)} %damping.1), custom_call_target="tpu_custom_call" | custom-call | tf_op jit(solution)/shard_map/pallas_call | solution.py:407
  45.7 1.5 %copy.10 = f32[2,1,1,96,128]{4,3,2,1,0:T(8,128)} copy(f32[2,1,1,96,128]{4,3,2,1,0:T(8,128)} %shard_map.64) | data formatting | bytes 196608

commit v3 on v2

--- a/solution.py
+++ b/solution.py
@@ -47,17 +47,33 @@
     return jnp.broadcast_to(x[k : k + 1, :], x.shape)
 
 
-def factor(x, start):
-    xr, xi = x
-    n = xr.shape[1]
-    lane = lax.broadcasted_iota(jnp.int32, (PANEL, n), 1) - start
+def lookahead(x, cols, z):
+    terms = []
+    for j, (cr, ci) in enumerate(cols):
+        rr, ri = row_bcast(z[0], j), row_bcast(z[1], j)
+        terms.append((cr * rr - ci * ri, cr * ri + ci * rr))
+    while len(terms) > 1:
+        terms = [(p[0] + q[0], p[1] + q[1]) for p, q in zip(terms[::2], terms[1::2])]
+    return x[0] - terms[0][0], x[1] - terms[0][1]
+
+
+def turned(x, start):
+    n = x[0].shape[1]
+    turn = (2 * n - start) % n
+    return pltpu.roll(x[0], turn, 1), pltpu.roll(x[1], turn, 1)
+
+
+def factor(x, front, start):
+    n = x[0].shape[1]
+    lane = lax.broadcasted_iota(jnp.int32, (PANEL, n), 1)
     sub = lax.broadcasted_iota(jnp.int32, (PANEL, n), 0)
-    turn = (n - start) % n
-    tr = pltpu.roll(xr, turn, 1)
-    ti = pltpu.roll(xi, turn, 1)
-    cols = [(lane_bcast(tr, j), lane_bcast(ti, j)) for j in range(PANEL)]
-    inside = (lane >= 0) & (lane < PANEL)
-    cols.append((jnp.where(inside, (lane == sub).astype(jnp.float32), xr), jnp.where(inside, 0.0, xi)))
+    cols = [(lane_bcast(front[0], j), lane_bcast(front[1], j)) for j in range(PANEL)]
+    ahead = turned(x, start + PANEL)
+    for (re, im), at in ((x, lane - start), (ahead, lane - (n - PANEL))):
+        inside = (at >= 0) & (at < PANEL)
+        cols.append(
+            (jnp.where(inside, (at == sub).astype(jnp.float32), re), jnp.where(inside, 0.0, im))
+        )
     for k in range(PANEL):
         br, bi = cols[k]
         pr, pi = row_bcast(br, k), row_bcast(bi, k)
@@ -66,14 +82,15 @@
         qr = jnp.where(here, -pr, br * pr + bi * pi)
         qi = jnp.where(here, pi, bi * pr - br * pi)
         mr, mi = qr * scale, qi * scale
-        for j in range(k + 1, PANEL + 1):
+        for j in range(k + 1, len(cols)):
             cr, ci = cols[j]
             rr, ri = row_bcast(cr, k), row_bcast(ci, k)
             cols[j] = (
                 jnp.where(here, 0.0, cr) - (mr * rr - mi * ri),
                 jnp.where(here, 0.0, ci) - (mr * ri + mi * rr),
             )
-    return cols[PANEL]
+    return cols[PANEL], cols[PANEL + 1]
+
 
 def invert(a, rhs):
     n = a.shape[0]
@@ -95,41 +112,46 @@
         keep = (wide < start) | (wide >= start + PANEL)
         return jnp.where(keep, old, 0.0) - dot(old, rhs[...])
 
-    def clear(start):
-        rows, low = places(start)
+    def columns(x, start):
+        side = turned(x, start)
+        return tuple((lane_bcast(side[0], j), lane_bcast(side[1], j)) for j in range(PANEL))
+
+    def without(x, start):
+        there = (lane >= start) & (lane < start + PANEL)
+        return tuple(jnp.where(there, 0.0, v) for v in x)
+
+    def following(start):
+        begin = pl.multiple_of(jnp.minimum(start + PANEL, n - PANEL), PANEL)
+        return halves(a[pl.ds(begin, PANEL), :])
+
+    def prepare(x, start):
+        front = tuple(jnp.where(lane >= n - PANEL, 0.0, v) for v in turned(x, start + PANEL))
+        return without(x, start), front, columns(x, start)
+
+    x = halves(a[:PANEL, :])
+    first = factor(x, x, 0)
+    put(0, first[0])
+
+    def block(b, carry):
+        (z, ahead), (x, front, cols) = carry
+        last = pl.multiple_of((b - 1) * PANEL, PANEL)
+        start = pl.multiple_of(b * PANEL, PANEL)
+        later = following(start)
+        later = lookahead(without(later, last), columns(later, last), z)
+        later = prepare(later, start)
+        new = updated(last)
+        x = lookahead(x, cols, z)
+        front = lookahead(front, cols, ahead)
+        fresh = factor(x, front, start)
+        a[...] = new
+        a[pl.ds(last, PANEL), :] = cat(z[0], z[1])
+        rows, low = places(last)
         rhs[rows, :] = zero
         rhs[low, :] = zero
-
-    first = factor(halves(a[:PANEL, :]), 0)
-    put(0, first)
-
-    def block(b, z):
-        last = pl.multiple_of((b - 1) * PANEL, PANEL)
-        start = pl.multiple_of(b * PANEL, PANEL)
-        new = updated(last)
-        xr, xi = halves(a[pl.ds(start, PANEL), :])
-        turn = (n - last) % n
-        tr = pltpu.roll(xr, turn, 1)
-        ti = pltpu.roll(xi, turn, 1)
-        inside = (lane >= last) & (lane < last + PANEL)
-        xr = jnp.where(inside, 0.0, xr)
-        xi = jnp.where(inside, 0.0, xi)
-        accs=[]
-        for j in range(PANEL):
-            cr, ci = lane_bcast(tr, j), lane_bcast(ti, j)
-            rr, ri = row_bcast(z[0], j), row_bcast(z[1], j)
-            accs.append((cr * rr - ci * ri, cr * ri + ci * rr))
-        while len(accs)>1:
-            accs=[(p[0]+q[0],p[1]+q[1]) for p,q in zip(accs[::2],accs[1::2])]
-        xr, xi = xr-accs[0][0], xi-accs[0][1]
-        fresh = factor((xr, xi), start)
-        a[...] = new
-        a[pl.ds(last, PANEL), :] = cat(z[0], z[1])
-        clear(last)
-        put(start, fresh)
-        return fresh
-
-    z = lax.fori_loop(1, n // PANEL, block, first)
+        put(start, fresh[0])
+        return fresh, later
+
+    (z, _), _ = lax.fori_loop(1, n // PANEL, block, (first, prepare(following(0), 0)))
     last = n - PANEL
     a[...] = updated(last)
     a[pl.ds(last, PANEL), :] = cat(z[0], z[1])

time: 47.5 us -> 44.3 us (0.933)
  Pallas kernels: 44.4 us -> 41.3 us
    pallas_call x1, Pallas kernels: 44.4 us -> 41.3 us  [local(): pl.pallas_call(functools.partial(kernel, regions, peers), in_specs=[SM, S...]
where the time goes in v3:
time: 44.3 us; the launch traced here: 44.2 us
  Pallas kernels  41.3 us (93%)
  local copies, waits for them, and re-layouts  1.54 us (3%)
  between operations  1.3 us (3%)
    pallas_call x1, Pallas kernels, local(): pl.pallas_call(functools.partial(kernel, regions, peers), in_specs=[SM, S...  41.3 us
    unnamed x1, local copies, waits for them, and re-layouts  1.54 us

profile of v3, /device:TPU:0, one launch (start us, length us, event | category | flops | bytes accessed | tf_op | source)
XLA Modules:
  0.0 44.2 jit_solution(2618718811542467266)
XLA Ops:
  1.3 41.3 %shard_map.64 = f32[2,1,1,96,128]{4,3,2,1,0:T(8,128)} custom-call(s32[1]{0:T(128)S(6)} %copy.9.sizes, f32[1,1]{1,0:T(1,128)S(6)} %copy.8.occ, s32[8]{0:T(128)} %offsets.1, f32[1,2,128,128]{3,2,1,0:T(8,128)} %onsite.1, f32[1,2,128,128]{3,2,1,0:T(8,128)} %coupling.1, f32[1,128]{1,0:T(1,128)} %damping.1), custom_call_target="tpu_custom_call" | custom-call | tf_op jit(solution)/shard_map/pallas_call | solution.py:429
  42.6 1.5 %copy.10 = f32[2,1,1,96,128]{4,3,2,1,0:T(8,128)} copy(f32[2,1,1,96,128]{4,3,2,1,0:T(8,128)} %shard_map.64) | data formatting | bytes 196608

commit v4 on v3

--- a/solution.py
+++ b/solution.py
@@ -217,7 +217,7 @@
 
 def kernel(
     regions, peers, sizes, occ, offsets, onsite, coupling, damping, out_ref,
-    a, g, w, u, u_in, s_out, s_in, m_out, m_in, g_in, full, rhs,
+    a, g, w, wh, u, uh, u_in, s_out, s_in, m_out, m_in, g_in, full, rhs,
     band_out, band_in, pol_out, pol_in,
     link_send, link_recv, band_send, band_recv, pol_send, pol_recv,
 ):
@@ -250,8 +250,9 @@
     lax.fori_loop(1, peers, greet_peer, 0)
 
     a0, u0 = build(regions, peers, sizes[0], onsite, coupling, damping)
+    u0h = adjoint(u0)
     u[...] = u0
-    w[...] = u0
+    uh[...] = u0h
     a[...] = a0
 
     gives = (pos >= half - 1) & (pos < regions - 1)
@@ -271,8 +272,22 @@
 
     @pl.when(pos == regions - 1)
     def _():
-        l_re, l_im = halves(cmul(u0, adjoint(u0)))
+        l_re, l_im = halves(cmul(u0, u0h))
         a[...] = a0 + cat(-l_im, l_re)
+
+    def below():
+        link(0, u, u_in, pos - 1).wait_recv()
+        w[...] = adjoint(u_in[...])
+        wh[...] = u_in[...]
+
+    @pl.when(left)
+    def _():
+        w[...] = u0
+        wh[...] = u0h
+
+    @pl.when(jnp.logical_not(left) & jnp.logical_not(is_end))
+    def _():
+        below()
 
     @pl.when(jnp.logical_not(is_end))
     def _():
@@ -284,8 +299,7 @@
 
         @pl.when(jnp.logical_not(left))
         def _():
-            uv = u[...]
-            a[...] = a[...] - cmul(cmul(uv, s_in[...]), adjoint(uv))
+            a[...] = a[...] - cmul(cmul(u[...], s_in[...]), uh[...])
 
     g[...] = a[...]
     invert(g, rhs)
@@ -300,13 +314,11 @@
             s_out[...] = g[...]
             own.start()
 
-        link(0, u, u_in, pos - 1).wait_recv()
-        w[...] = adjoint(u_in[...])
+        pl.when(is_end)(below)
 
     @pl.when(is_mid)
     def _():
-        wv = w[...]
-        m_out[...] = cmul(cmul(adjoint(wv), g[...]), wv)
+        m_out[...] = cmul(cmul(wh[...], g[...]), w[...])
         copy = link(2, m_out, m_in, inner)
         copy.start()
         copy.wait_recv()
@@ -317,7 +329,7 @@
     @pl.when(jnp.logical_not(is_mid))
     def _():
         wv = w[...]
-        wg = cmul(adjoint(wv), g[...])
+        wg = cmul(wh[...], g[...])
 
         @pl.when(left)
         def _():
@@ -386,26 +398,23 @@
             acc = lax.fori_loop(0, peers, term, acc)
         return energy_step * acc[0], energy_step * acc[1]
 
+    def owner_values(owner):
+        return jnp.concatenate([v for i in range(kept) for v in frequency(owner, i)], axis=0)
+
     def owned(j, carry):
         owner = lax.rem(me + j, peers)
-        for i in range(kept):
-            re, im = frequency(owner, i)
-            pol_out[owner, i, 0] = re
-            pol_out[owner, i, 1] = im
-
+        pol_out[owner] = owner_values(owner)
         pol_copy(j).start()
         return carry
 
     lax.fori_loop(1, peers, owned, 0)
-    for i in range(kept):
-        re, im = frequency(me, i)
-        pol_in[me, i, 0] = re
-        pol_in[me, i, 1] = im
+    pol_in[me] = owner_values(me)
     each(pol_copy, lambda c: c.wait_recv())
     for e in range(peers):
         for i in range(kept):
             for c in range(2):
-                out_ref[c, i, 0, e * rows : (e + 1) * rows, :] = pol_in[e, i, c]
+                begin = (2 * i + c) * rows
+                out_ref[c, i, 0, e * rows : (e + 1) * rows, :] = pol_in[e, begin : begin + rows]
 
     each(band_copy, lambda c: c.wait_send())
     each(pol_copy, lambda c: c.wait_send())
@@ -431,13 +440,13 @@
         in_specs=[SM, SM, SM, VM, VM, VM],
         out_specs=VM,
         out_shape=jax.ShapeDtypeStruct((2, kept, 1, BAND, n), jnp.float32),
-        scratch_shapes=[block] * 11
+        scratch_shapes=[block] * 13
         + [
             pltpu.VMEM((2 * n, 2 * n), jnp.float32),
             pltpu.VMEM((peers, 4, rows, n), jnp.bfloat16),
             pltpu.VMEM((peers, 4, rows, n), jnp.bfloat16),
-            pltpu.VMEM((peers, kept, 2, rows, n), jnp.float32),
-            pltpu.VMEM((peers, kept, 2, rows, n), jnp.float32),
+            pltpu.VMEM((peers, 2 * kept * rows, n), jnp.float32),
+            pltpu.VMEM((peers, 2 * kept * rows, n), jnp.float32),
             pltpu.SemaphoreType.DMA((4,)),
             pltpu.SemaphoreType.DMA((4,)),
         ]

time: 44.3 us -> 44.2 us (level)
  no operation moved by 1% of the time
where the time goes in v4:
time: 44.2 us; the launch traced here: 44 us
  Pallas kernels  41.1 us (93%)
  local copies, waits for them, and re-layouts  1.54 us (3%)
  between operations  1.3 us (3%)
    pallas_call x1, Pallas kernels, local(): pl.pallas_call(functools.partial(kernel, regions, peers), in_specs=[SM, S...  41.1 us
    unnamed x1, local copies, waits for them, and re-layouts  1.54 us

profile of v4, /device:TPU:0, one launch (start us, length us, event | category | flops | bytes accessed | tf_op | source)
XLA Modules:
  0.0 44.0 jit_solution(13378765610805814540)
XLA Ops:
  1.3 41.1 %shard_map.64 = f32[2,1,1,96,128]{4,3,2,1,0:T(8,128)} custom-call(s32[1]{0:T(128)S(6)} %copy.9.sizes, f32[1,1]{1,0:T(1,128)S(6)} %copy.8.occ, s32[8]{0:T(128)} %offsets.1, f32[1,2,128,128]{3,2,1,0:T(8,128)} %onsite.1, f32[1,2,128,128]{3,2,1,0:T(8,128)} %coupling.1, f32[1,128]{1,0:T(1,128)} %damping.1), custom_call_target="tpu_custom_call" | custom-call | tf_op jit(solution)/shard_map/pallas_call | solution.py:438
  42.4 1.5 %copy.10 = f32[2,1,1,96,128]{4,3,2,1,0:T(8,128)} copy(f32[2,1,1,96,128]{4,3,2,1,0:T(8,128)} %shard_map.64) | data formatting | bytes 196608
